TPU v7x, 32 devices: a whole 2x2x4 slice. The times are simulated.
32 devices in a mesh: grp: 4 (over y, x), dev: 8 (over z, core).
Axes of the slice: x: 2, y: 2, z: 4, core: 2. Of those that a mesh axis runs over, the one named last changes fastest.
Arguments:
- q_lat: bfloat16 [128, 64, 576], P(('grp', 'dev')), parts along dimension 0, may hold values from -40 to 40
- latent_cache: bfloat16 [128, 256, 576], P(('grp', 'dev')), parts along dimension 0, may hold values from -8 to 8
- lengths: int32 [128], P('grp'), parts along dimension 0, may hold values from 32 to 256, as said below
- moves: int32 [64, 3], P('grp'), parts along dimension 0, may hold values from 0 to 31, as said below
- hidden_in: bfloat16 [128, 3584], P(('grp', 'dev')), parts along dimension 0, may hold values from -6 to 6
- norm_gain: bfloat16 [3584], replicated, may hold values from 0.25 to 1.75
- w_up: bfloat16 [3584, 10240], P(None, 'dev'), may hold values from -0.09375 to 0.09375
- w_down: bfloat16 [10240, 3584], P('dev'), may hold values from -0.0625 to 0.0625
- queue_counts: int32 [32, 8], P(('grp', 'dev')), parts along dimension 0, may hold values from 0 to 63
- deadline: int32 [128], P(('grp', 'dev')), parts along dimension 0, may hold values from 0 to 7
Outputs:
- attn_out: bfloat16 [128, 64, 512], P(('grp', 'dev')), parts along dimension 0
- new_cache: bfloat16 [128, 256, 576], P(('grp', 'dev')), parts along dimension 0
- mixed: bfloat16 [128, 3584], P(('grp', 'dev')), parts along dimension 0
- bucket_load: float32 [32], P('grp'), parts along dimension 0
There are 4 independent parts, one for each index of `grp`. A program takes and returns all parts, laid end to end along the dimension named above; an argument that names none is the same for every part. Nothing has to cross between parts.
Inputs may be any that keep to these rules, and one draw needn't show every extreme that they name: `lengths`: every length is at least 32; some request has exactly 256. `moves`: entry j * 8 + s (j below 2) has source device s and names a request of device s (requests r lie on device r // 4); the requests listed for one device are distinct. In round j every source s sends to (s + k_j) mod 8, with k_j between 1 and 7 the same for all sources of the round and different between rounds; one of the rounds has k_j = 4.
All inputs are finite; a program needn't handle non-finite values.
Results may differ from a plain program's by a relative error of at most 0.002.
The roundings to bfloat16 on the way count: a program that leaves them out, or rounds other values in their place, can miss the bound.
Values may be sent and summed in bfloat16 or wider, within the bound.
A program may use at most 128 MiB of HBM per device.

v0:
```python
from functools import partial
import jax
import jax.numpy as jnp
from jax import lax
from jax.sharding import PartitionSpec as P

VL = 512
MOVE_DEV = 2
BUCKETS = 8
softmax_scale = 192.0 ** (-0.5)


def for_sending(x):

    def short(part):
        return part.astype(jnp.bfloat16) if part.dtype == jnp.float32 else part

    return jax.tree.map(short, x)


def shifted(value, axis, steps):
    count = lax.axis_size(axis)
    pairs = [(source, (source + steps) % count) for source in range(count)]
    return lax.ppermute(value, axis, pairs)


def attend(queries, latent, context_lengths):
    row_count = queries.shape[0]
    head_count = queries.shape[1]
    block_size = min(128, latent.shape[1])
    block_count = (jnp.max(context_lengths) + block_size - 1) // block_size
    initial = (
        jnp.full((row_count, head_count), -1e30, jnp.float32),
        jnp.zeros((row_count, head_count), jnp.float32),
        jnp.zeros((row_count, head_count, VL), jnp.float32),
    )

    def advance(block_index, carried):
        running_max, running_sum, accumulated = carried
        key_block = lax.dynamic_slice_in_dim(latent, block_index * block_size, block_size, 1)
        scores = (
            jnp.einsum("rhc,rkc->rhk", queries, key_block, preferred_element_type=jnp.float32)
            * softmax_scale
        )
        positions = block_index * block_size + jnp.arange(block_size, dtype=jnp.int32)
        included = positions[None, None, :] < context_lengths[:, None, None]
        scores = jnp.where(included, scores, jnp.float32(-1e30))
        new_max = jnp.maximum(running_max, jnp.max(scores, axis=-1))
        factor = jnp.exp(running_max - new_max)
        weights = jnp.where(included, jnp.exp(scores - new_max[:, :, None]), jnp.float32(0.0))
        running_sum = running_sum * factor + jnp.sum(weights, axis=-1)
        product = jnp.einsum(
            "rhk,rkc->rhc",
            weights.astype(jnp.bfloat16),
            key_block[:, :, :VL],
            preferred_element_type=jnp.float32,
        )
        accumulated = accumulated * factor[:, :, None] + product
        return (new_max, running_sum, accumulated)

    final_max, final_sum, accumulated = lax.fori_loop(0, block_count, advance, initial)
    return (accumulated / final_sum[:, :, None]).astype(jnp.bfloat16)


def moved_by(offset, single_row):
    return jax.tree.map(
        lambda part, own: part.astype(own.dtype),
        shifted(for_sending(single_row), "dev", offset),
        single_row,
    )


def send_round(single_row, round_distance, devices):
    branches = [partial(moved_by, offset) for offset in range(1, devices)]
    return lax.switch(round_distance - 1, branches, single_row)


def per_device(
    q_lat, latent_cache, lengths, moves, hidden_in, norm_gain, w_up, w_down, queue_counts, deadline
):
    devices = lax.axis_size("dev")
    my_index = lax.axis_index("dev")
    row_count = latent_cache.shape[0]
    context = latent_cache.shape[1]
    rounds = moves.reshape(MOVE_DEV, devices, 3)
    own_moves = rounds[:, my_index, :]
    leaving = own_moves[:, 0] - my_index * row_count
    distance = (own_moves[:, 2] - my_index) % devices
    own_lengths = lax.dynamic_slice_in_dim(lengths, my_index * row_count, row_count)
    payload = latent_cache[leaving]
    arrivals = []
    for round_index in range(MOVE_DEV):
        arrivals.append(send_round(payload[round_index], distance[round_index], devices))
    travelled = jnp.stack(arrivals, axis=0)
    new_cache = latent_cache.at[leaving].set(travelled[:, :context])
    attn_out = attend(q_lat, latent_cache, own_lengths)
    widened = hidden_in.astype(jnp.float32)
    scaled = lax.rsqrt(jnp.mean(widened * widened, axis=-1, keepdims=True) + 1e-06)
    normed = (widened * scaled * norm_gain.astype(jnp.float32)[None, :]).astype(jnp.bfloat16)
    running = (deadline[:, None] == jnp.arange(BUCKETS, dtype=jnp.int32)[None, :]).astype(
        jnp.float32
    )
    bucket_terms = queue_counts.astype(jnp.float32)[0] + jnp.sum(running, axis=0)
    all_rows = lax.all_gather(normed, "dev", axis=0, tiled=True)
    bucket_load = lax.psum(bucket_terms, "dev")
    hidden_units = jax.nn.silu(jnp.dot(all_rows, w_up, preferred_element_type=jnp.float32)).astype(
        jnp.bfloat16
    )
    partial_sum = lax.psum_scatter(
        jnp.dot(hidden_units, w_down, preferred_element_type=jnp.float32),
        "dev",
        scatter_dimension=0,
        tiled=True,
    )
    mixed = (widened + partial_sum).astype(jnp.bfloat16)
    return (attn_out, new_cache, mixed, bucket_load)


def solution(mesh):
    return jax.shard_map(
        per_device,
        mesh=mesh,
        in_specs=(
            P(("grp", "dev"), None, None),
            P(("grp", "dev"), None, None),
            P("grp"),
            P("grp", None),
            P(("grp", "dev"), None),
            P(),
            P(None, "dev"),
            P("dev", None),
            P(("grp", "dev"), None),
            P(("grp", "dev")),
        ),
        out_specs=(
            P(("grp", "dev"), None, None),
            P(("grp", "dev"), None, None),
            P(("grp", "dev"), None),
            P("grp"),
        ),
        check_vma=False,
    )
```

profile of v0, /device:TPU:0, one launch (start us, length us, event | category | flops | bytes accessed | tf_op | source)
XLA Modules:
  0.0 112.7 jit_solution(7425908061489002161)
XLA Ops:
  7.2 0.6 copy-done.4
  8.2 16.0 %all-gather = bf16[8,4,3584]{2,1,0:T(4,128)(2,1)S(1)} all-gather(bf16[1,4,3584]{2,1,0:T(4,128)(2,1)S(1)} %fusion.19), channel_id=1, replica_groups=mesh['grp'=4,'dev'=8] {'dev'}, dimensions={0}, use_global_device_ids=true | all-gather | bytes 258048 | tf_op jit(solution)/shard_map/all_gather | solution.py:104
  24.2 10.4 %fusion.13 = f32[32,3584]{1,0:T(8,128)} fusion(bf16[1280,3584]{1,0:T(8,128)(2,1)} %param.33, bf16[32,3584]{1,0:T(8,128)(2,1)S(1)} %reshape.87, bf16[3584,1280]{1,0:T(8,128)(2,1)} %param.32), kind=kOutput, calls=%fused_computation.41 | convolution fusion | flops 587407360 | bytes 19038208 | tf_op jit(solution)/shard_map/dot_general | solution.py:110
  34.7 0.7 fusion.23
  36.2 1.0 while.14
  36.3 0.3 fusion.40
  36.7 0.2 fusion.41
  36.9 0.4 convolution_add_fusion.2
  37.7 0.6 fusion.25
  38.3 0.6 gather_fusion
  38.9 0.3 copy.53
  40.5 16.7 %conditional.3 = (bf16[1,256,576]{2,1,0:T(8,128)(2,1)}) conditional(s32[]{:T(128)} %bitcast.31, bf16[2,256,576]{2,1,0:T(8,128)(2,1)S(1)} %copy.53, bf16[2,256,576]{2,1,0:T(8,128)(2,1)S(1)} %copy.53, bf16[2,256,576]{2,1,0:T(8,128)(2,1)S(1)} %copy.53, bf16[2,256,576]{2,1,0:T(8,128)(2,1)S(1)} %copy.53, ...), branch_computations={%region_12.13_spmd, %region_13.14_spmd, %region_14.15_spmd, %regio... | conditional | bytes 1769520 | solution.py:75
  40.6 2.5 %collective-permute-start.9 = (bf16[256,576]{1,0:T(8,128)(2,1)S(1)}, bf16[256,576]{1,0:T(8,128)(2,1)}, u32[]{:S(2)}, u32[]{:S(2)}) collective-permute-start(bf16[256,576]{1,0:T(8,128)(2,1)S(1)} %slice_bitcast_fusion.9), channel_id=1, source_target_pairs={{0,3},{1,4},{2,5},{3,6},{4,7},{5,0},{6,1},{7,2},{8,11},{9,12},{10,... | collective-permute-start | bytes 884744 | tf_op jit(solution)/shard_map/cond/branch_2_fun/ppermute | solution.py:24
  43.1 14.1 %collective-permute-done.9 = bf16[256,576]{1,0:T(8,128)(2,1)} collective-permute-done((bf16[256,576]{1,0:T(8,128)(2,1)S(1)}, bf16[256,576]{1,0:T(8,128)(2,1)}, u32[]{:S(2)}, u32[]{:S(2)}) %collective-permute-start.9) | collective-permute-done | bytes 294944 | tf_op jit(solution)/shard_map/cond/branch_2_fun/ppermute | solution.py:24
  57.2 16.8 %conditional.2 = (bf16[1,256,576]{2,1,0:T(8,128)(2,1)}) conditional(s32[]{:T(128)} %bitcast.30, bf16[2,256,576]{2,1,0:T(8,128)(2,1)S(1)} %copy.53, bf16[2,256,576]{2,1,0:T(8,128)(2,1)S(1)} %copy.53, bf16[2,256,576]{2,1,0:T(8,128)(2,1)S(1)} %copy.53, bf16[2,256,576]{2,1,0:T(8,128)(2,1)S(1)} %copy.53, ...), branch_computations={%region_5.6_spmd, %region_6.7_spmd, %region_7.8_spmd, %region_8.9_... | conditional | bytes 1769520 | solution.py:75
  57.4 16.7 %collective-permute-done.3 = bf16[256,576]{1,0:T(8,128)(2,1)} collective-permute-done((bf16[256,576]{1,0:T(8,128)(2,1)S(1)}, bf16[256,576]{1,0:T(8,128)(2,1)}, u32[]{:S(2)}, u32[]{:S(2)}) %collective-permute-start.3) | collective-permute-done | bytes 294944 | tf_op jit(solution)/shard_map/cond/branch_3_fun/ppermute | solution.py:24
  74.2 1.2 %pad_maximum_fusion = bf16[2,256,576]{2,1,0:T(8,128)(2,1)S(1)} fusion(bf16[1,256,576]{2,1,0:T(8,128)(2,1)} %get-tuple-element.231, bf16[1,256,576]{2,1,0:T(8,128)(2,1)} %get-tuple-element.230), kind=kLoop, calls=%fused_computation.35 | loop fusion | flops 294912 | bytes 1179648 | tf_op jit(solution)/shard_map/stack | solution.py:94
  75.4 0.2 copy.67
  75.6 14.2 %psum.7 = f32[8]{0:T(128)} all-reduce(f32[8]{0:T(128)S(1)} %bitcast_add_fusion), channel_id=1, replica_groups=mesh['grp'=4,'dev'=8] {'dev'}, use_global_device_ids=true, to_apply=%region_23.24 | all-reduce | flops 8 | bytes 64 | tf_op jit(solution)/shard_map/psum | solution.py:105
  89.8 0.8 scatter_fusion
  90.6 0.7 dynamic-slice
  92.0 0.8 divide_convert_fusion
  92.8 11.5 %all-reduce.3.cloned.1.call-done = f32[32,3584]{1,0:T(8,128)} async-done(((f32[32,3584]{1,0:T(8,128)}), f32[32,3584]{1,0:T(8,128)}) %all-reduce.3.cloned.1.call-update) | async-done | bytes 458768
  104.3 1.5 %fusion.18 = bf16[4,3584]{1,0:T(4,128)(2,1)} fusion(bf16[4,3584]{1,0:T(4,128)(2,1)S(1)} %copy-done.3, f32[32,3584]{1,0:T(8,128)} %all-reduce.3.cloned.1.call-done, u32[]{:T(128)S(6)} %multiply.7), kind=kLoop, calls=%fused_computation.46 | loop fusion | flops 43008 | bytes 114692 | tf_op jit(solution)/shard_map/convert_element_type | solution.py:115
  (45 shorter events, 1.3 us)
Async XLA Ops:
  7.2 0.7 copy-start.3
  7.2 0.7 copy-start.4
  7.2 97.2 %all-reduce.3.cloned.1.call-start = ((), (), s32[]{:S(2)}) async-start(), calls=%async_computation | async-start | bytes 917504
  24.2 10.5 %copy-start.6 = (s32[32]{0:T(128)S(1)}, s32[32]{0:T(128)}, u32[]{:S(2)}) copy-start(s32[32]{0:T(128)} %param.28) | copy-start | bytes 388
  24.2 12.0 %copy-start.1 = (bf16[4,256,576]{1,2,0:T(8,128)(2,1)S(1)}, bf16[4,256,576]{1,2,0:T(8,128)(2,1)}, u32[]{:S(2)}) copy-start(bf16[4,256,576]{1,2,0:T(8,128)(2,1)} %param.27) | copy-start | bytes 3538948
  24.2 12.0 %copy-start.2 = (bf16[4,64,576]{2,1,0:T(8,128)(2,1)S(1)}, bf16[4,64,576]{2,1,0:T(8,128)(2,1)}, u32[]{:S(2)}) copy-start(bf16[4,64,576]{2,1,0:T(8,128)(2,1)} %param.26) | copy-start | bytes 884740
  36.2 1.1 copy-start.5
  40.6 16.7 %collective-permute-start.9 = (bf16[256,576]{1,0:T(8,128)(2,1)S(1)}, bf16[256,576]{1,0:T(8,128)(2,1)}, u32[]{:S(2)}, u32[]{:S(2)}) collective-permute-start(bf16[256,576]{1,0:T(8,128)(2,1)S(1)} %slice_bitcast_fusion.9), channel_id=1, source_target_pairs={{0,3},{1,4},{2,5},{3,6},{4,7},{5,0},{6,1},{7,2},{8,11},{9,12},{10,... | collective-permute-start | bytes 884744 | tf_op jit(solution)/shard_map/cond/branch_2_fun/ppermute | solution.py:24
  57.2 16.8 %copy-start.7 = (s32[4]{0:T(128)S(1)}, s32[4]{0:T(128)}, u32[]{:S(2)}) copy-start(s32[4]{0:T(128)} %param.35) | copy-start | bytes 52
  57.3 16.8 %collective-permute-start.3 = (bf16[256,576]{1,0:T(8,128)(2,1)S(1)}, bf16[256,576]{1,0:T(8,128)(2,1)}, u32[]{:S(2)}, u32[]{:S(2)}) collective-permute-start(bf16[256,576]{1,0:T(8,128)(2,1)S(1)} %slice_bitcast_fusion.3), channel_id=1, source_target_pairs={{0,4},{1,5},{2,6},{3,7},{4,0},{5,1},{6,2},{7,3},{8,12},{9,13},{10,... | collective-permute-start | bytes 884744 | tf_op jit(solution)/shard_map/cond/branch_3_fun/ppermute | solution.py:24
  74.1 1.3 %copy-start.8 = (s32[1,8]{1,0:T(1,128)S(1)}, s32[1,8]{1,0:T(1,128)}, u32[]{:S(2)}) copy-start(s32[1,8]{1,0:T(1,128)} %param.34) | copy-start | bytes 100
  75.6 15.0 %copy-start.9 = (u32[32]{0:T(128)S(1)}, u32[32]{0:T(128)}, u32[]{:S(2)}) copy-start(u32[32]{0:T(128)} %constant.94) | copy-start | bytes 388
  90.6 15.3 %copy-start = (bf16[4,256,576]{1,2,0:T(8,128)(2,1)}, bf16[4,256,576]{1,2,0:T(8,128)(2,1)S(1)}, u32[]{:S(2)}) copy-start(bf16[4,256,576]{1,2,0:T(8,128)(2,1)S(1)} %scatter_fusion) | copy-start | bytes 3538948
Sparse Core Ops, SparseCore 0:
  34.8 69.4 all-reduce.2
where the time goes:
time: 113 us
  waiting for transfers between devices  42.4 us (38%)
  blocking collectives  30.2 us (27%)
  between operations  16.9 us (15%)
  matrix products  11.1 us (10%)
  other arithmetic  5.04 us (4%)
  local copies, waits for them, and re-layouts  4.32 us (4%)
  starting transfers between devices  2.65 us (2%)
    ppermute x2, waiting for transfers between devices, shifted(): return lax.ppermute(value, axis, pairs)  30.8 us
    all_gather x1, blocking collectives, per_device(): all_rows = lax.all_gather(normed, 'dev', axis=0, tiled=True)  16 us
    psum x1, blocking collectives, per_device(): bucket_load = lax.psum(bucket_terms, 'dev')  14.2 us
    unnamed x2, waiting for transfers between devices  11.6 us
    dot_general x1, matrix products, per_device(): jnp.dot(hidden_units, w_down, preferred_element_type=jnp.float32)  10.4 us
    ppermute x2, starting transfers between devices, shifted(): return lax.ppermute(value, axis, pairs)  2.61 us
  transfers between devices with their start and end apart: 3, of which 3 were waited for; matrix products, arithmetic and copies ran while one was open for 7% of the time, Pallas kernels for 0%

commit v1 on v0

--- a/solution.py
+++ b/solution.py
@@ -102,7 +102,11 @@
     )
     bucket_terms = queue_counts.astype(jnp.float32)[0] + jnp.sum(running, axis=0)
     all_rows = lax.all_gather(normed, "dev", axis=0, tiled=True)
-    bucket_load = lax.psum(bucket_terms, "dev")
+    bucket_load = bucket_terms
+    for hop in (1, 2, 4):
+        bucket_load = bucket_load + lax.ppermute(
+            bucket_load, "dev", [(dev, dev ^ hop) for dev in range(8)]
+        )
     hidden_units = jax.nn.silu(jnp.dot(all_rows, w_up, preferred_element_type=jnp.float32)).astype(
         jnp.bfloat16
     )

time: 113 us -> 113 us (level)
  blocking collectives: 30.2 us -> 16 us
  waiting for transfers between devices: 42.4 us -> 56 us
    psum x1 -> x0, blocking collectives: 14.2 us -> none  [per_device(): bucket_load = lax.psum(bucket_terms, 'dev')]
    ppermute x0 -> x3, waiting for transfers between devices: none -> 7.9 us  [per_device(): lax.ppermute(bucket_load, 'dev', [(dev, dev ^ hop) for dev in range(8)])]
    unnamed x2, waiting for transfers between devices: 11.6 us -> 17.4 us
  transfers between devices with their start and end apart: 3 -> 6, of which waited for: 3 -> 5; matrix products, arithmetic and copies ran while one was open for 7% -> 7% of each run, Pallas kernels for 0% -> 0%
where the time goes in v1:
time: 113 us
  waiting for transfers between devices  56 us (50%)
  between operations  16.9 us (15%)
  blocking collectives  16 us (14%)
  matrix products  11.1 us (10%)
  other arithmetic  5.56 us (5%)
  local copies, waits for them, and re-layouts  4.33 us (4%)
  starting transfers between devices  3.01 us (3%)
    ppermute x2, waiting for transfers between devices, shifted(): return lax.ppermute(value, axis, pairs)  30.7 us
    unnamed x2, waiting for transfers between devices  17.4 us
    all_gather x1, blocking collectives, per_device(): all_rows = lax.all_gather(normed, 'dev', axis=0, tiled=True)  16 us
    dot_general x1, matrix products, per_device(): jnp.dot(hidden_units, w_down, preferred_element_type=jnp.float32)  10.4 us
    ppermute x3, waiting for transfers between devices, per_device(): lax.ppermute(bucket_load, 'dev', [(dev, dev ^ hop) for dev in range(8)])  7.9 us
    ppermute x2, starting transfers between devices, shifted(): return lax.ppermute(value, axis, pairs)  2.43 us
  transfers between devices with their start and end apart: 6, of which 5 were waited for; matrix products, arithmetic and copies ran while one was open for 7% of the time, Pallas kernels for 0%

profile of v1, /device:TPU:0, one launch (start us, length us, event | category | flops | bytes accessed | tf_op | source)
XLA Modules:
  0.0 113.0 jit_solution(5462535165990947602)
XLA Ops:
  7.2 0.6 copy-done.4
  8.2 16.0 %all-gather = bf16[8,4,3584]{2,1,0:T(4,128)(2,1)S(1)} all-gather(bf16[1,4,3584]{2,1,0:T(4,128)(2,1)S(1)} %fusion.19), channel_id=1, replica_groups=mesh['grp'=4,'dev'=8] {'dev'}, dimensions={0}, use_global_device_ids=true | all-gather | bytes 258048 | tf_op jit(solution)/shard_map/all_gather | solution.py:104
  24.2 10.4 %fusion.13 = f32[32,3584]{1,0:T(8,128)} fusion(bf16[1280,3584]{1,0:T(8,128)(2,1)} %param.33, bf16[32,3584]{1,0:T(8,128)(2,1)S(1)} %reshape.87, bf16[3584,1280]{1,0:T(8,128)(2,1)} %param.32), kind=kOutput, calls=%fused_computation.41 | convolution fusion | flops 587407360 | bytes 19038208 | tf_op jit(solution)/shard_map/dot_general | solution.py:114
  34.8 0.4 collective-permute-start.14
  35.2 0.7 fusion.23
  36.7 1.0 while.14
  36.8 0.3 fusion.40
  37.4 0.4 convolution_add_fusion.2
  38.3 0.6 fusion.25
  38.9 0.6 gather_fusion
  41.1 16.6 %conditional.3 = (bf16[1,256,576]{2,1,0:T(8,128)(2,1)}) conditional(s32[]{:T(128)} %bitcast.31, bf16[2,256,576]{2,1,0:T(8,128)(2,1)S(1)} %copy.53, bf16[2,256,576]{2,1,0:T(8,128)(2,1)S(1)} %copy.53, bf16[2,256,576]{2,1,0:T(8,128)(2,1)S(1)} %copy.53, bf16[2,256,576]{2,1,0:T(8,128)(2,1)S(1)} %copy.53, ...), branch_computations={%region_12.13_spmd, %region_13.14_spmd, %region_14.15_spmd, %regio... | conditional | bytes 1769520 | solution.py:75
  41.1 2.4 %collective-permute-start.9 = (bf16[256,576]{1,0:T(8,128)(2,1)S(1)}, bf16[256,576]{1,0:T(8,128)(2,1)}, u32[]{:S(2)}, u32[]{:S(2)}) collective-permute-start(bf16[256,576]{1,0:T(8,128)(2,1)S(1)} %slice_bitcast_fusion.9), channel_id=1, source_target_pairs={{0,3},{1,4},{2,5},{3,6},{4,7},{5,0},{6,1},{7,2},{8,11},{9,12},{10,... | collective-permute-start | bytes 884744 | tf_op jit(solution)/shard_map/cond/branch_2_fun/ppermute | solution.py:24
  43.5 14.1 %collective-permute-done.9 = bf16[256,576]{1,0:T(8,128)(2,1)} collective-permute-done((bf16[256,576]{1,0:T(8,128)(2,1)S(1)}, bf16[256,576]{1,0:T(8,128)(2,1)}, u32[]{:S(2)}, u32[]{:S(2)}) %collective-permute-start.9) | collective-permute-done | bytes 294944 | tf_op jit(solution)/shard_map/cond/branch_2_fun/ppermute | solution.py:24
  57.6 16.7 %conditional.2 = (bf16[1,256,576]{2,1,0:T(8,128)(2,1)}) conditional(s32[]{:T(128)} %bitcast.30, bf16[2,256,576]{2,1,0:T(8,128)(2,1)S(1)} %copy.53, bf16[2,256,576]{2,1,0:T(8,128)(2,1)S(1)} %copy.53, bf16[2,256,576]{2,1,0:T(8,128)(2,1)S(1)} %copy.53, bf16[2,256,576]{2,1,0:T(8,128)(2,1)S(1)} %copy.53, ...), branch_computations={%region_5.6_spmd, %region_6.7_spmd, %region_7.8_spmd, %region_8.9_... | conditional | bytes 1769520 | solution.py:75
  57.7 16.6 %collective-permute-done.3 = bf16[256,576]{1,0:T(8,128)(2,1)} collective-permute-done((bf16[256,576]{1,0:T(8,128)(2,1)S(1)}, bf16[256,576]{1,0:T(8,128)(2,1)}, u32[]{:S(2)}, u32[]{:S(2)}) %collective-permute-start.3) | collective-permute-done | bytes 294944 | tf_op jit(solution)/shard_map/cond/branch_3_fun/ppermute | solution.py:24
  74.3 1.2 %pad_maximum_fusion = bf16[2,256,576]{2,1,0:T(8,128)(2,1)S(1)} fusion(bf16[1,256,576]{2,1,0:T(8,128)(2,1)} %get-tuple-element.231, bf16[1,256,576]{2,1,0:T(8,128)(2,1)} %get-tuple-element.230), kind=kLoop, calls=%fused_computation.35 | loop fusion | flops 294912 | bytes 1179648 | tf_op jit(solution)/shard_map/stack | solution.py:94
  75.8 0.8 scatter_fusion
  76.6 0.7 dynamic-slice
  77.9 0.8 divide_convert_fusion
  78.7 3.6 %collective-permute-done.15 = f32[8]{0:T(128)S(1)} collective-permute-done((f32[8]{0:T(128)S(1)}, f32[8]{0:T(128)S(1)}, u32[]{:S(2)}, u32[]{:S(2)}) %collective-permute-start.15) | collective-permute-done | bytes 64 | tf_op jit(solution)/shard_map/ppermute | solution.py:107
  82.4 4.3 %collective-permute-done.16 = f32[8]{0:T(128)S(1)} collective-permute-done((f32[8]{0:T(128)S(1)}, f32[8]{0:T(128)S(1)}, u32[]{:S(2)}, u32[]{:S(2)}) %collective-permute-start.16) | collective-permute-done | bytes 64 | tf_op jit(solution)/shard_map/ppermute | solution.py:107
  86.8 0.5 add.87
  87.3 17.3 %all-reduce.3.cloned.1.call-done = f32[32,3584]{1,0:T(8,128)} async-done(((f32[32,3584]{1,0:T(8,128)}), f32[32,3584]{1,0:T(8,128)}) %all-reduce.3.cloned.1.call-update) | async-done | bytes 458768
  104.6 1.5 %fusion.18 = bf16[4,3584]{1,0:T(4,128)(2,1)} fusion(bf16[4,3584]{1,0:T(4,128)(2,1)S(1)} %copy-done.3, f32[32,3584]{1,0:T(8,128)} %all-reduce.3.cloned.1.call-done, u32[]{:T(128)S(6)} %multiply.7), kind=kLoop, calls=%fused_computation.46 | loop fusion | flops 43008 | bytes 114692 | tf_op jit(solution)/shard_map/convert_element_type | solution.py:119
  (53 shorter events, 2.1 us)
Async XLA Ops:
  7.2 0.7 copy-start.3
  7.2 0.7 copy-start.4
  7.2 97.4 %all-reduce.3.cloned.1.call-start = ((), (), s32[]{:S(2)}) async-start(), calls=%async_computation | async-start | bytes 917504
  24.2 10.5 %copy-start.7 = (s32[4]{0:T(128)S(1)}, s32[4]{0:T(128)}, u32[]{:S(2)}) copy-start(s32[4]{0:T(128)} %param.35) | copy-start | bytes 52
  24.2 10.6 %copy-start.8 = (s32[1,8]{1,0:T(1,128)S(1)}, s32[1,8]{1,0:T(1,128)}, u32[]{:S(2)}) copy-start(s32[1,8]{1,0:T(1,128)} %param.34) | copy-start | bytes 100
  24.2 11.0 %copy-start.6 = (s32[32]{0:T(128)S(1)}, s32[32]{0:T(128)}, u32[]{:S(2)}) copy-start(s32[32]{0:T(128)} %param.28) | copy-start | bytes 388
  24.2 12.5 %copy-start.1 = (bf16[4,256,576]{1,2,0:T(8,128)(2,1)S(1)}, bf16[4,256,576]{1,2,0:T(8,128)(2,1)}, u32[]{:S(2)}) copy-start(bf16[4,256,576]{1,2,0:T(8,128)(2,1)} %param.27) | copy-start | bytes 3538948
  24.2 12.5 %copy-start.2 = (bf16[4,64,576]{2,1,0:T(8,128)(2,1)S(1)}, bf16[4,64,576]{2,1,0:T(8,128)(2,1)}, u32[]{:S(2)}) copy-start(bf16[4,64,576]{2,1,0:T(8,128)(2,1)} %param.26) | copy-start | bytes 884740
  34.8 43.9 %collective-permute-start.14 = (f32[8]{0:T(128)S(1)}, f32[8]{0:T(128)S(1)}, u32[]{:S(2)}, u32[]{:S(2)}) collective-permute-start(f32[8]{0:T(128)S(1)} %bitcast_add_fusion), channel_id=1, source_target_pairs={{0,1},{1,0},{2,3},{3,2},{4,5},{5,4},{6,7},{7,6},{8,9},{9,8},{10,11... | collective-permute-start | bytes 104 | tf_op jit(solution)/shard_map/ppermute | solution.py:107
  36.7 1.1 copy-start.5
  41.1 16.5 %collective-permute-start.9 = (bf16[256,576]{1,0:T(8,128)(2,1)S(1)}, bf16[256,576]{1,0:T(8,128)(2,1)}, u32[]{:S(2)}, u32[]{:S(2)}) collective-permute-start(bf16[256,576]{1,0:T(8,128)(2,1)S(1)} %slice_bitcast_fusion.9), channel_id=1, source_target_pairs={{0,3},{1,4},{2,5},{3,6},{4,7},{5,0},{6,1},{7,2},{8,11},{9,12},{10,... | collective-permute-start | bytes 884744 | tf_op jit(solution)/shard_map/cond/branch_2_fun/ppermute | solution.py:24
  57.7 16.7 %collective-permute-start.3 = (bf16[256,576]{1,0:T(8,128)(2,1)S(1)}, bf16[256,576]{1,0:T(8,128)(2,1)}, u32[]{:S(2)}, u32[]{:S(2)}) collective-permute-start(bf16[256,576]{1,0:T(8,128)(2,1)S(1)} %slice_bitcast_fusion.3), channel_id=1, source_target_pairs={{0,4},{1,5},{2,6},{3,7},{4,0},{5,1},{6,2},{7,3},{8,12},{9,13},{10,... | collective-permute-start | bytes 884744 | tf_op jit(solution)/shard_map/cond/branch_3_fun/ppermute | solution.py:24
  75.7 0.8 copy-start.9
  76.5 29.6 %copy-start = (bf16[4,256,576]{1,2,0:T(8,128)(2,1)}, bf16[4,256,576]{1,2,0:T(8,128)(2,1)S(1)}, u32[]{:S(2)}) copy-start(bf16[4,256,576]{1,2,0:T(8,128)(2,1)S(1)} %scatter_fusion) | copy-start | bytes 3538948
  78.7 3.6 %collective-permute-start.15 = (f32[8]{0:T(128)S(1)}, f32[8]{0:T(128)S(1)}, u32[]{:S(2)}, u32[]{:S(2)}) collective-permute-start(f32[8]{0:T(128)S(1)} %add.85), channel_id=1, source_target_pairs={{0,2},{1,3},{2,0},{3,1},{4,6},{5,7},{6,4},{7,5},{8,10},{9,11},{10,... | collective-permute-start | bytes 104 | tf_op jit(solution)/shard_map/ppermute | solution.py:107
  82.3 4.5 %collective-permute-start.16 = (f32[8]{0:T(128)S(1)}, f32[8]{0:T(128)S(1)}, u32[]{:S(2)}, u32[]{:S(2)}) collective-permute-start(f32[8]{0:T(128)S(1)} %add.86), channel_id=1, source_target_pairs={{0,4},{1,5},{2,6},{3,7},{4,0},{5,1},{6,2},{7,3},{8,12},{9,13},{10,... | collective-permute-start | bytes 104 | tf_op jit(solution)/shard_map/ppermute | solution.py:107
Sparse Core Ops, SparseCore 0:
  34.8 69.7 all-reduce.2
